TPU v7x, 32 devices: a whole 2x2x4 slice. The times are simulated.
32 devices in a mesh: groups: 2 (over y), chol: 4 (over z), walk: 4 (over x, core).
Axes of the slice: x: 2, y: 2, z: 4, core: 2. Of those that a mesh axis runs over, the one named last changes fastest.
Arguments:
- green: bfloat16 [8, 200, 1600], P(('groups', 'walk')), parts along dimension 0, may hold values from -2 to 2
- chol: bfloat16 [16, 200, 1600], P(('groups', 'chol')), parts along dimension 0, may hold values from -0.19921875 to 0.19921875
- trial: bfloat16 [3200, 200], P(('groups', 'chol')), parts along dimension 0, may hold values from -1.1953125 to 1.1953125
- hamil: bfloat16 [1600, 1600], P('chol'), may hold values from -0.21875 to 0.21875
- energy_cot: float32 [8], P('groups'), parts along dimension 0, may hold values from -4 to 4
Outputs:
- d_green: float32 [8, 200, 1600], P(('groups', 'walk'), None, 'chol'), parts along dimension 0
- d_chol: float32 [16, 200, 1600], P(('groups', 'chol'), None, 'walk'), parts along dimension 0
- d_trial: float32 [3200, 200], P(('groups', 'chol')), parts along dimension 0
There are 2 independent parts, one for each index of `groups`. A program takes and returns all parts, laid end to end along the dimension named above; an argument that names none is the same for every part. Nothing has to cross between parts.
All inputs are finite; a program needn't handle non-finite values.
Results may differ from a plain program's by a relative error of at most 0.0029.
Values may be sent and summed in bfloat16 or wider, within the bound.
No kernel may reach another device: no remote copies, remote signals or barrier semaphores. Data moves between devices by JAX's collectives and lax.ppermute only.
A program may use at most 64 MiB of HBM per device.

v0:
```python
import functools

import jax
import jax.numpy as jnp
from jax import lax
from jax.experimental import pallas as pl
from jax.experimental.pallas import tpu as pltpu
from jax.sharding import PartitionSpec as P


F32 = jnp.float32
BF16 = jnp.bfloat16
LANES = 128
SUBLANES = 8
MIB = 1024 * 1024


def plain(green, chol, trial, hamil, energy_cot):
    walk_rank = lax.axis_index("walk")
    walk_rows = green.shape[0]
    cot_own = lax.dynamic_slice_in_dim(energy_cot, walk_rank * walk_rows, walk_rows, 0)
    hrot_part = lax.dot_general(
        trial, hamil, (((0,), (0,)), ((), ())), preferred_element_type=F32
    )
    identity = jnp.eye(trial.shape[1], dtype=F32)
    quarter = green.shape[2] // lax.axis_size("walk")
    greens = lax.all_gather(green, "walk", axis=0, tiled=True)
    coulomb = jnp.einsum("cip,wip->cw", chol, greens, preferred_element_type=F32)
    exchange_mat = jnp.einsum("cip,wjp->cwij", chol, greens, preferred_element_type=F32)
    kernel_mat = (
        energy_cot[None, :, None, None] * (coulomb[:, :, None, None] * identity - exchange_mat)
    ).astype(BF16)
    kernel_own = lax.dynamic_slice_in_dim(kernel_mat, walk_rank * walk_rows, walk_rows, 1)
    green_part = jnp.einsum("cwij,cjp->wip", kernel_own, chol, preferred_element_type=F32)
    green_part = green_part + cot_own[:, None, None] * hrot_part[None]
    d_green = lax.psum_scatter(green_part, "chol", scatter_dimension=2, tiled=True)
    green_share = lax.dynamic_slice_in_dim(greens, walk_rank * quarter, quarter, 2)
    d_chol = jnp.einsum("cwji,wjp->cip", kernel_mat, green_share, preferred_element_type=F32)
    gbar = jnp.einsum(
        "w,wip->ip",
        energy_cot,
        greens,
        precision=lax.Precision.HIGHEST,
        preferred_element_type=F32,
    ).astype(BF16)
    d_trial = lax.dot_general(hamil, gbar, (((1,), (1,)), ((), ())), preferred_element_type=F32)
    return (d_green, d_chol, d_trial)


def nn(a, b):
    return jnp.dot(a, b, preferred_element_type=F32)


def nt(a, b):
    return lax.dot_general(a, b, (((1,), (1,)), ((), ())), preferred_element_type=F32)


def kernel_of(exch, cot):
    row = lax.broadcasted_iota(jnp.int32, exch.shape, 0)
    col = lax.broadcasted_iota(jnp.int32, exch.shape, 1)
    on_diagonal = jnp.where(row == col, exch, 0.0)
    coul = jnp.sum(jnp.sum(on_diagonal, axis=0, keepdims=True), axis=1, keepdims=True)
    return (cot * jnp.where(row == col, coul - exch, -exch)).astype(BF16)


def row_groups(rows, width):
    fits = [n for n in range(1, rows + 1) if rows % n == 0 and rows // n % SUBLANES == 0]
    padded = {n: -(-n * width // LANES) * LANES / n for n in fits}
    least = min(padded.values())
    return min(n for n in fits if padded[n] <= 1.03 * least)


def half_of(half, kernel_ref, cot, chol_ref, trial_ref, hamil_ref, part_ref, packed_ref, groups):
    nocc, norb = chol_ref.shape[1:]
    width = norb // 4
    height = nocc // groups
    skew = 2 * width % LANES
    size = 2 * width + skew
    window = pl.ds(pl.multiple_of(half * (2 * width - skew), LANES), size)
    total = cot * nn(trial_ref[...].T, hamil_ref[:, window])
    for v in range(chol_ref.shape[0]):
        total += nn(kernel_ref[v], chol_ref[v, :, window])
    part_ref[:, :size] = total
    for place in range(2):

        @pl.when(half == place)
        def _():
            for q in range(2):
                left = place * skew + q * width
                for r in range(groups):
                    packed_ref[q, :, r * width : (r + 1) * width] = part_ref[
                        r * height : (r + 1) * height, left : left + width
                    ]


def crossing_kernel(groups, *refs):
    _, green_ref, chol_ref, cot_in, trial_in, hamil_in = refs[:6]
    second_ref, third_ref, kept_ref, paired_ref, kernel_ref, trial_ref, hamil_ref = refs[6:13]
    cot_ref, part_ref, packed_ref, sems = refs[13:]
    cut = second_ref.shape[0]
    cot_copy = pltpu.make_async_copy(cot_in, cot_ref, sems.at[0])
    trial_copy = pltpu.make_async_copy(trial_in, trial_ref, sems.at[1])
    hamil_copy = pltpu.make_async_copy(hamil_in, hamil_ref, sems.at[2])
    cot_copy.start()
    trial_copy.start()
    hamil_copy.start()
    vectors = chol_ref.shape[0]
    rank = lax.axis_index("chol")
    exchange = [nt(chol_ref[v], green_ref[0]) for v in range(vectors)]
    cot_copy.wait()
    cot = cot_ref[lax.axis_index("walk")]
    for v in range(vectors):
        kernel_ref[v] = kernel_of(exchange[v], cot)
    trial_copy.wait()
    hamil_copy.wait()
    half_of(
        1 - rank // 2, kernel_ref, cot, chol_ref, trial_ref, hamil_ref, part_ref, packed_ref, groups
    )
    second_ref[...] = packed_ref[rank % 2, :cut].astype(BF16)
    third_ref[...] = packed_ref[1 - rank % 2, :cut].astype(BF16)
    kept_ref[...] = packed_ref[rank % 2, cut:]
    paired_ref[...] = packed_ref[1 - rank % 2, cut:].astype(BF16)


def staying_kernel(groups, *refs):
    cot_ref, kernel_ref, chol_ref, trial_ref, hamil_ref = refs[:5]
    first_ref, own_ref, part_ref, packed_ref = refs[5:]
    rank = lax.axis_index("chol")
    cot = cot_ref[lax.axis_index("walk")]
    half_of(
        rank // 2, kernel_ref, cot, chol_ref, trial_ref, hamil_ref, part_ref, packed_ref, groups
    )
    first_ref[...] = packed_ref[1 - rank % 2].astype(BF16)
    own_ref[...] = packed_ref[rank % 2]


def half_scratch(nocc, norb, block):
    wide = -(-(norb // 2) // LANES) * LANES + LANES
    return [pltpu.VMEM((nocc, wide), F32), pltpu.VMEM((2,) + block, F32)]


def shape_of(x):
    return jax.ShapeDtypeStruct(x.shape, x.dtype)


def opening_kernel(out_ref):
    out_ref[...] = jnp.zeros_like(out_ref)


def opening():
    return pl.pallas_call(
        opening_kernel,
        out_shape=jax.ShapeDtypeStruct((SUBLANES, LANES), F32),
        out_specs=pl.BlockSpec(memory_space=pltpu.VMEM),
        cost_estimate=pl.CostEstimate(flops=4 * 10**9, bytes_accessed=4096, transcendentals=0),
        compiler_params=pltpu.CompilerParams(vmem_limit_bytes=MIB, has_side_effects=True),
        name="opening",
    )()


def crossing(groups, cut, token, cot, green, chol, trial, hamil):
    _, nocc, norb = green.shape
    vectors = chol.shape[0]
    block = (nocc // groups, groups * (norb // 4))
    rest = (block[0] - cut, block[1])
    vmem = pl.BlockSpec(memory_space=pltpu.VMEM)
    loaded = [pltpu.with_memory_space_constraint(x, pltpu.HBM) for x in (cot, trial, hamil)]
    return pl.pallas_call(
        functools.partial(crossing_kernel, groups),
        out_shape=[jax.ShapeDtypeStruct((cut, block[1]), BF16)] * 2
        + [jax.ShapeDtypeStruct(rest, F32), jax.ShapeDtypeStruct(rest, BF16)]
        + [jax.ShapeDtypeStruct((vectors, nocc, nocc), BF16), shape_of(trial), shape_of(hamil)],
        in_specs=[vmem] * 3 + [pl.BlockSpec(memory_space=pltpu.HBM)] * 3,
        out_specs=[vmem] * 7,
        scratch_shapes=[pltpu.SMEM(cot.shape, F32)]
        + half_scratch(nocc, norb, block)
        + [pltpu.SemaphoreType.DMA((3,))],
        cost_estimate=pl.CostEstimate(
            flops=nocc * norb * (3 * vectors * nocc + trial.shape[0]),
            bytes_accessed=2 * (green.size + chol.size + trial.size + hamil.size),
            transcendentals=0,
        ),
        compiler_params=pltpu.CompilerParams(vmem_limit_bytes=16 * MIB),
        name="crossing",
    )(token, green, chol, *loaded)


def staying(groups, cot, kernels, chol, trial, hamil):
    vectors, nocc, norb = chol.shape
    block = (nocc // groups, groups * (norb // 4))
    vmem = pl.BlockSpec(memory_space=pltpu.VMEM)
    return pl.pallas_call(
        functools.partial(staying_kernel, groups),
        out_shape=[jax.ShapeDtypeStruct(block, BF16), jax.ShapeDtypeStruct(block, F32)],
        in_specs=[pl.BlockSpec(memory_space=pltpu.SMEM)] + [vmem] * 4,
        out_specs=[vmem] * 2,
        scratch_shapes=half_scratch(nocc, norb, block),
        cost_estimate=pl.CostEstimate(
            flops=nocc * norb * (vectors * nocc + trial.shape[0]),
            bytes_accessed=2 * (chol.size + trial.size + hamil.size),
            transcendentals=0,
        ),
        compiler_params=pltpu.CompilerParams(vmem_limit_bytes=16 * MIB),
        name="staying",
    )(cot, kernels, chol, trial, hamil)


def unpacked_rows(out_ref, packed_ref, groups):
    height, width = packed_ref.shape[0], packed_ref.shape[1] // groups
    for r in range(groups):
        out_ref[r * height : (r + 1) * height, :] = packed_ref[:, r * width : (r + 1) * width]


def share_of(rank, norb, ways):
    width = norb // ways
    offsets = [w * width % LANES for w in range(ways)]
    begin = rank * width // LANES * LANES
    return pl.ds(pl.multiple_of(begin, LANES), width + max(offsets)), rank * width - begin


def window_size(norb, ways):
    width = norb // ways
    return width + max(w * width % LANES for w in range(ways))


def call(kernel, out_shape, args, flops, moved, **more):
    vmem = pl.BlockSpec(memory_space=pltpu.VMEM)
    smem = pl.BlockSpec(memory_space=pltpu.SMEM)
    return pl.pallas_call(
        kernel,
        out_shape=out_shape,
        in_specs=[smem if x.ndim == 1 else vmem for x in args],
        cost_estimate=pl.CostEstimate(flops=flops, bytes_accessed=moved, transcendentals=0),
        compiler_params=pltpu.CompilerParams(vmem_limit_bytes=16 * MIB),
        **{"out_specs": [vmem] * len(out_shape), **more},
    )(*args)


def pair_kernel(kept_ref, received_ref, out_ref):
    out_ref[...] = (kept_ref[...] + received_ref[...].astype(F32)).astype(BF16)


def pair_sum(kept, received):
    out = [shape_of(received)]
    return call(pair_kernel, out, (kept, received), kept.size, 8 * kept.size)[0]


def early_kernel(ways, cot_ref, chol_ref, hamil_ref, green_ref, near_ref, kernel_ref, *outs):
    d_chol_ref, d_trial_ref = outs
    rank = lax.axis_index("walk")
    vectors, _, norb = chol_ref.shape
    window, _ = share_of(rank, norb, ways)
    flipped = [nt(near_ref[0], chol_ref[v]) for v in range(chol_ref.shape[0])]
    total = cot_ref[rank] * nt(hamil_ref[...], green_ref[0])
    d_trial_ref[...] = total + cot_ref[rank ^ 1] * nt(hamil_ref[...], near_ref[0])
    for v in range(vectors):
        own = nn(kernel_ref[v].T, green_ref[0, :, window])
        near = kernel_of(flipped[v], cot_ref[rank ^ 1])
        d_chol_ref[v] = own + nn(near, near_ref[0, :, window])


def middle_kernel(bits, ways, cot_ref, chol_ref, hamil_ref, green_ref, *refs):
    old_chol, old_trial, d_chol_ref, d_trial_ref = refs
    rank = lax.axis_index("walk")
    cot = cot_ref[rank ^ bits]
    vectors, _, norb = chol_ref.shape
    window, _ = share_of(rank, norb, ways)
    flipped = [nt(green_ref[0], chol_ref[v]) for v in range(chol_ref.shape[0])]
    d_trial_ref[...] = old_trial[...] + cot * nt(hamil_ref[...], green_ref[0])
    for v in range(vectors):
        kernel = kernel_of(flipped[v], cot)
        d_chol_ref[v] = old_chol[v] + nn(kernel, green_ref[0, :, window])


def walkers(kernel, ways, cot, chol, hamil, greens, *rest):
    vectors, nocc, norb = chol.shape
    size = window_size(norb, ways)
    return call(
        kernel,
        [
            jax.ShapeDtypeStruct((vectors, nocc, size), F32),
            jax.ShapeDtypeStruct((hamil.shape[0], nocc), F32),
        ],
        (cot, chol, hamil, *greens, *rest),
        2 * nocc * len(greens) * (nocc * vectors * (norb + size) + hamil.size),
        2 * (chol.size + len(greens) * nocc * norb),
    )


def late_kernel(bits, ways, cot_ref, chol_ref, hamil_ref, green_ref, *refs):
    old_chol, old_trial, d_chol_ref, d_trial_ref, wide_ref = refs
    rank = lax.axis_index("walk")
    cot = cot_ref[rank ^ bits]
    vectors, _, norb = chol_ref.shape
    window, offset = share_of(rank, norb, ways)
    flipped = [nt(green_ref[0], chol_ref[v]) for v in range(vectors)]
    d_trial_ref[...] = old_trial[...] + cot * nt(hamil_ref[...], green_ref[0])
    for v in range(vectors):
        kernel = kernel_of(flipped[v], cot)
        total = old_chol[v] + nn(kernel, green_ref[0, :, window])
        wide_ref[v, :, : total.shape[1]] = total
        moved = pltpu.roll(wide_ref[v], wide_ref.shape[2] - offset, 1)
        d_chol_ref[v] = moved[:, : norb // ways]


def late(bits, ways, cot, chol, hamil, green, old):
    vectors, nocc, norb = chol.shape
    wide = -(-window_size(norb, ways) // LANES) * LANES
    shapes = [(vectors, nocc, norb // ways), (hamil.shape[0], nocc)]
    return call(
        functools.partial(late_kernel, bits, ways),
        [jax.ShapeDtypeStruct(shape, F32) for shape in shapes],
        (cot, chol, hamil, green, *old),
        2 * nocc * (nocc * vectors * (norb + wide) + hamil.size),
        2 * (chol.size + hamil.size + nocc * norb),
        scratch_shapes=[pltpu.VMEM((vectors, nocc, wide), F32)],
    )


def joined_kernel(groups, cut, chol_ref, trial_ref, *refs):
    own_ref, first_ref, second_ref, third_ref, pair_ref = refs[:5]
    green_out, chol_out, trial_out, sum_ref, d_green, sems = refs[5:]
    copies = [
        pltpu.make_async_copy(trial_ref, trial_out, sems.at[1]),
        pltpu.make_async_copy(chol_ref, chol_out, sems.at[2]),
    ]
    for copy in copies:
        copy.start()
    total = own_ref[...] + first_ref[...].astype(F32)
    sum_ref[:cut] = total[:cut] + second_ref[...].astype(F32) + third_ref[...].astype(F32)
    sum_ref[cut:] = total[cut:] + pair_ref[...].astype(F32)
    unpacked_rows(d_green.at[0], sum_ref, groups)
    copies.append(pltpu.make_async_copy(d_green, green_out, sems.at[0]))
    copies[-1].start()
    for copy in copies:
        copy.wait()


def joined(groups, cut, d_chol, d_trial, own, received):
    height, long = own.shape
    shape = (1, groups * height, long // groups)
    return call(
        functools.partial(joined_kernel, groups, cut),
        [jax.ShapeDtypeStruct(shape, F32), shape_of(d_chol), shape_of(d_trial)],
        (d_chol, d_trial, own, *received),
        own.size * 4,
        own.size * 16,
        out_specs=[pl.BlockSpec(memory_space=pltpu.HBM)] * 3,
        scratch_shapes=[
            pltpu.VMEM((height, long), F32),
            pltpu.VMEM(shape, F32),
            pltpu.SemaphoreType.DMA((3,)),
        ],
    )


def swapped(x, axis, bits):
    return lax.ppermute(x, axis, [(i, i ^ bits) for i in range(lax.axis_size(axis))])


def shards(green, chol, trial, hamil, energy_cot):
    ways = lax.axis_size("walk")
    _, nocc, norb = green.shape
    groups = row_groups(nocc, norb // lax.axis_size("chol"))
    cut = nocc // groups * 2 // 5 // SUBLANES * SUBLANES
    far = swapped(green, "walk", 2)
    token = opening()
    second, third, kept, paired, kernels, trial, hamil = crossing(
        groups, cut, token, energy_cot, green, chol, trial, hamil
    )
    paired = swapped(paired, "chol", 1)
    second = swapped(second, "chol", 2)
    third = swapped(third, "chol", 3)
    near = swapped(green, "walk", 1)
    both = swapped(pair_sum(kept, paired), "chol", 2)
    first, own = staying(groups, energy_cot, kernels, chol, trial, hamil)
    first = swapped(first, "chol", 1)
    early = functools.partial(early_kernel, ways)
    same = (ways, energy_cot, chol, hamil)
    sums = walkers(early, *same, [green, near], kernels)
    other = swapped(far, "walk", 1)
    middle = functools.partial(middle_kernel, 2, ways)
    sums = walkers(middle, *same, [far], *sums)
    sums = late(3, *same, other, sums)
    return tuple(joined(groups, cut, *sums, own, (first, second, third, both)))


def solution(mesh):
    fits = mesh.shape["walk"] == 4 and mesh.shape["chol"] == 4

    def body(green, *rest):
        if fits and green.shape[0] == 1 and green.shape[1] % SUBLANES == 0:
            return shards(green, *rest)
        return plain(green, *rest)

    return jax.shard_map(
        body,
        mesh=mesh,
        in_specs=(
            P(("groups", "walk"), None, None),
            P(("groups", "chol"), None, None),
            P(("groups", "chol"), None),
            P("chol", None),
            P("groups"),
        ),
        out_specs=(
            P(("groups", "walk"), None, "chol"),
            P(("groups", "chol"), None, "walk"),
            P(("groups", "chol"), None),
        ),
        check_vma=False,
    )
```

profile of v0, /device:TPU:0, one launch (start us, length us, event | category | flops | bytes accessed | tf_op | source)
XLA Modules:
  0.0 41.5 jit_solution(11746615991363371850)
XLA Ops:
  0.6 0.0 copy-start.1
  0.6 0.0 copy-start
  0.6 3.0 %collective-permute-start = (bf16[1,200,1600]{2,1,0:T(8,128)(2,1)}, bf16[1,200,1600]{2,1,0:T(8,128)(2,1)S(1)}, u32[]{:S(2)}, u32[]{:S(2)}) collective-permute-start(bf16[1,200,1600]{2,1,0:T(8,128)(2,1)} %green_ref.1), channel_id=1, source_target_pairs={{0,2},{1,3},{2,0},{3,1},{4,6},{5,7},{6,4},{7,5},{8,10},{9,11},{10,... | collective-permute-start | bytes 1920008 | tf_op jit(solution)/shard_map/ppermute | solution.py:358
  3.7 0.0 collective-permute-start.2
  3.7 15.2 %collective-permute-done.green_ref = bf16[1,200,1600]{2,1,0:T(8,128)(2,1)S(1)} collective-permute-done((bf16[1,200,1600]{2,1,0:T(8,128)(2,1)}, bf16[1,200,1600]{2,1,0:T(8,128)(2,1)S(1)}, u32[]{:S(2)}, u32[]{:S(2)}) %collective-permute-start) | collective-permute-done | bytes 640032 | tf_op jit(solution)/shard_map/ppermute | solution.py:358
  18.8 0.0 collective-permute-start.1
  18.8 0.0 copy-done.1
  18.9 0.0 copy-done
  18.9 0.0 copy-start.2
  18.9 2.7 %crossing.1 = (bf16[16,2000]{1,0:T(8,128)(2,1)S(1)}, bf16[16,2000]{1,0:T(8,128)(2,1)S(1)}, f32[24,2000]{1,0:T(8,128)S(1)}, bf16[24,2000]{1,0:T(8,128)(2,1)S(1)},...) custom-call(f32[8,128]{1,0:T(8,128)S(1)} %opening.1.refs_0_, ...), custom_call_target="tpu_custom_call" | custom-call | flops 512000000 | bytes 3360000 | tf_op jit(solution)/shard_map/crossing/pallas_call | solution.py:168
  21.6 1.9 %collective-permute-start.6 = (bf16[24,2000]{1,0:T(8,128)(2,1)S(1)}, bf16[24,2000]{1,0:T(8,128)(2,1)S(1)}, u32[]{:S(2)}, u32[]{:S(2)}) collective-permute-start(bf16[24,2000]{1,0:T(8,128)(2,1)S(1)} %get-tuple-element.32), channel_id=1, source_target_pairs={{0,4},{4,0},{8,12},{12,8},{1,5},{5,1},{9,13},{13,9},{2,6},{6,2},{1... | collective-permute-start | bytes 288008 | tf_op jit(solution)/shard_map/ppermute | solution.py:358
  23.5 0.0 copy-done.2
  23.5 1.4 %staying.1 = (bf16[40,2000]{1,0:T(8,128)(2,1)S(1)}, f32[40,2000]{1,0:T(8,128)S(1)}) custom-call(f32[4]{0:T(128)S(1)} %copy-done.2, bf16[2,200,200]{2,1,0:T(8,128)(2,1)S(1)} %get-tuple-element.19.kernel_ref.refs_1_, bf16[2,200,1600]{2,1,0:T(8,128)(2,1)S(1)} %copy-done, bf16[400,200]{1,0:T(8,128)(2,1)S(1)} %get-tuple-element.26.refs_3_, ...), custom_call_target="tpu_custom_call" | custom-call | flops 256000000 | bytes 2720000 | tf_op jit(solution)/shard_map/staying/pallas_call | solution.py:192
  25.0 0.3 collective-permute-start.3
  25.2 2.8 %collective-permute-start.4 = (bf16[16,2000]{1,0:T(8,128)(2,1)S(1)}, bf16[16,2000]{1,0:T(8,128)(2,1)S(1)}, u32[]{:S(2)}, u32[]{:S(2)}) collective-permute-start(bf16[16,2000]{1,0:T(8,128)(2,1)S(1)} %get-tuple-element.29), channel_id=1, source_target_pairs={{0,8},{4,12},{8,0},{12,4},{1,9},{5,13},{9,1},{13,5},{2,10},{6,14},... | collective-permute-start | bytes 192008 | tf_op jit(solution)/shard_map/ppermute | solution.py:358
  28.1 0.0 collective-permute-done.6.received_ref
  28.1 3.1 %collective-permute-start.5 = (bf16[16,2000]{1,0:T(8,128)(2,1)S(1)}, bf16[16,2000]{1,0:T(8,128)(2,1)S(1)}, u32[]{:S(2)}, u32[]{:S(2)}) collective-permute-start(bf16[16,2000]{1,0:T(8,128)(2,1)S(1)} %get-tuple-element.30), channel_id=1, source_target_pairs={{0,12},{4,8},{8,4},{12,0},{1,13},{5,9},{9,5},{13,1},{2,14},{6,10},... | collective-permute-start | bytes 192008 | tf_op jit(solution)/shard_map/ppermute | solution.py:358
  31.2 0.0 collective-permute-done.2.near_ref
  31.2 0.1 collective-permute-start.7
  31.3 2.1 %shard_map.76 = (f32[2,200,448]{2,1,0:T(8,128)S(1)}, f32[400,200]{1,0:T(8,128)S(1)}) custom-call(f32[4]{0:T(128)S(1)} %copy-done.2, bf16[2,200,1600]{2,1,0:T(8,128)(2,1)S(1)} %copy-done, bf16[400,1600]{1,0:T(8,128)(2,1)S(1)} %get-tuple-element.18.hamil_ref.refs_4_, bf16[1,200,1600]{2,1,0:T(8,128)(2,1)S(1)} %copy-done.1, ...), custom_call_target="tpu_custom_call" | custom-call | flops 1167360000 | bytes 2560000 | tf_op jit(solution)/shard_map/pallas_call | solution.py:229
  33.4 1.6 %shard_map.77 = (f32[2,200,448]{2,1,0:T(8,128)S(1)}, f32[400,200]{1,0:T(8,128)S(1)}) custom-call(f32[4]{0:T(128)S(1)} %copy-done.2, bf16[2,200,1600]{2,1,0:T(8,128)(2,1)S(1)} %copy-done, bf16[400,1600]{1,0:T(8,128)(2,1)S(1)} %get-tuple-element.18.hamil_ref.refs_4_, bf16[1,200,1600]{2,1,0:T(8,128)(2,1)S(1)} %collective-permute-done.green_ref, ...), custom_call_target="tpu_custom_call" | custom-call | flops 583680000 | bytes 1920000 | tf_op jit(solution)/shard_map/pallas_call | solution.py:229
  35.0 0.0 collective-permute-done.1.green_ref
  35.0 1.7 %shard_map.78 = (f32[2,200,400]{2,1,0:T(8,128)S(1)}, f32[400,200]{1,0:T(8,128)S(1)}) custom-call(f32[4]{0:T(128)S(1)} %copy-done.2, bf16[2,200,1600]{2,1,0:T(8,128)(2,1)S(1)} %copy-done, bf16[400,1600]{1,0:T(8,128)(2,1)S(1)} %get-tuple-element.18.hamil_ref.refs_4_, bf16[1,200,1600]{2,1,0:T(8,128)(2,1)S(1)} %collective-permute-done.1.green_ref, ...), custom_call_target="tpu_custom_call" | custom-call | flops 593920000 | bytes 3200000 | tf_op jit(solution)/shard_map/pallas_call | solution.py:229
  36.8 0.0 collective-permute-done.4.refs_2_
  36.8 0.3 collective-permute-done.5.refs_3_
  37.0 0.0 collective-permute-done.3.refs_1_
  37.0 3.3 %collective-permute-done.7.refs_4_ = bf16[24,2000]{1,0:T(8,128)(2,1)S(1)} collective-permute-done((bf16[24,2000]{1,0:T(8,128)(2,1)S(1)}, bf16[24,2000]{1,0:T(8,128)(2,1)S(1)}, u32[]{:S(2)}, u32[]{:S(2)}) %collective-permute-start.7) | collective-permute-done | bytes 96032 | tf_op jit(solution)/shard_map/ppermute | solution.py:358
  40.4 1.2 %shard_map.80 = (f32[1,200,400]{2,1,0:T(8,128)}, f32[2,200,400]{2,1,0:T(8,128)}, f32[400,200]{1,0:T(8,128)}) custom-call(f32[2,200,400]{2,1,0:T(8,128)S(1)} %get-tuple-element.24.chol_ref, f32[400,200]{1,0:T(8,128)S(1)} %get-tuple-element.25.trial_ref, f32[40,2000]{1,0:T(8,128)S(1)} %get-tuple-element.27.refs_0_, ...), custom_call_target="tpu_custom_call" | custom-call | flops 320000 | bytes 1280000 | tf_op jit(solution)/shard_map/pallas_call | solution.py:229
  (2 shorter events, 0.0 us)
Async XLA Ops:
  0.6 18.2 %copy-start.1 = (bf16[1,200,1600]{2,1,0:T(8,128)(2,1)S(1)}, bf16[1,200,1600]{2,1,0:T(8,128)(2,1)}, u32[]{:S(2)}) copy-start(bf16[1,200,1600]{2,1,0:T(8,128)(2,1)} %green_ref.1) | copy-start | bytes 1920004
  0.6 18.2 %copy-start = (bf16[2,200,1600]{2,1,0:T(8,128)(2,1)S(1)}, bf16[2,200,1600]{2,1,0:T(8,128)(2,1)}, u32[]{:S(2)}) copy-start(bf16[2,200,1600]{2,1,0:T(8,128)(2,1)} %refs_2_.3) | copy-start | bytes 3840004
  0.6 18.2 %collective-permute-start = (bf16[1,200,1600]{2,1,0:T(8,128)(2,1)}, bf16[1,200,1600]{2,1,0:T(8,128)(2,1)S(1)}, u32[]{:S(2)}, u32[]{:S(2)}) collective-permute-start(bf16[1,200,1600]{2,1,0:T(8,128)(2,1)} %green_ref.1), channel_id=1, source_target_pairs={{0,2},{1,3},{2,0},{3,1},{4,6},{5,7},{6,4},{7,5},{8,10},{9,11},{10,... | collective-permute-start | bytes 1920008 | tf_op jit(solution)/shard_map/ppermute | solution.py:358
  3.7 27.5 %collective-permute-start.2 = (bf16[1,200,1600]{2,1,0:T(8,128)(2,1)}, bf16[1,200,1600]{2,1,0:T(8,128)(2,1)S(1)}, u32[]{:S(2)}, u32[]{:S(2)}) collective-permute-start(bf16[1,200,1600]{2,1,0:T(8,128)(2,1)} %green_ref.1), channel_id=1, source_target_pairs={{0,1},{1,0},{2,3},{3,2},{4,5},{5,4},{6,7},{7,6},{8,9},{9,8},{10,11... | collective-permute-start | bytes 1920008 | tf_op jit(solution)/shard_map/ppermute | solution.py:358
  18.8 16.1 %collective-permute-start.1 = (bf16[1,200,1600]{2,1,0:T(8,128)(2,1)S(1)}, bf16[1,200,1600]{2,1,0:T(8,128)(2,1)S(1)}, u32[]{:S(2)}, u32[]{:S(2)}) collective-permute-start(bf16[1,200,1600]{2,1,0:T(8,128)(2,1)S(1)} %collective-permute-done.green_ref), channel_id=1, source_target_pairs={{0,1},{1,0},{2,3},{3,2},{4,5},{5,4},{6,7},{7,6},{8,9},{9,8},{10,11... | collective-permute-start | bytes 1920008 | tf_op jit(solution)/shard_map/ppermute | solution.py:358
  18.9 4.7 %copy-start.2 = (f32[4]{0:T(128)S(1)}, f32[4]{0:T(128)}, u32[]{:S(2)}) copy-start(f32[4]{0:T(128)} %refs_0_.1) | copy-start | bytes 52
  21.6 6.4 %collective-permute-start.6 = (bf16[24,2000]{1,0:T(8,128)(2,1)S(1)}, bf16[24,2000]{1,0:T(8,128)(2,1)S(1)}, u32[]{:S(2)}, u32[]{:S(2)}) collective-permute-start(bf16[24,2000]{1,0:T(8,128)(2,1)S(1)} %get-tuple-element.32), channel_id=1, source_target_pairs={{0,4},{4,0},{8,12},{12,8},{1,5},{5,1},{9,13},{13,9},{2,6},{6,2},{1... | collective-permute-start | bytes 288008 | tf_op jit(solution)/shard_map/ppermute | solution.py:358
  25.0 12.1 %collective-permute-start.3 = (bf16[40,2000]{1,0:T(8,128)(2,1)S(1)}, bf16[40,2000]{1,0:T(8,128)(2,1)S(1)}, u32[]{:S(2)}, u32[]{:S(2)}) collective-permute-start(bf16[40,2000]{1,0:T(8,128)(2,1)S(1)} %get-tuple-element.28), channel_id=1, source_target_pairs={{0,4},{4,0},{8,12},{12,8},{1,5},{5,1},{9,13},{13,9},{2,6},{6,2},{1... | collective-permute-start | bytes 480008 | tf_op jit(solution)/shard_map/ppermute | solution.py:358
  25.2 11.5 %collective-permute-start.4 = (bf16[16,2000]{1,0:T(8,128)(2,1)S(1)}, bf16[16,2000]{1,0:T(8,128)(2,1)S(1)}, u32[]{:S(2)}, u32[]{:S(2)}) collective-permute-start(bf16[16,2000]{1,0:T(8,128)(2,1)S(1)} %get-tuple-element.29), channel_id=1, source_target_pairs={{0,8},{4,12},{8,0},{12,4},{1,9},{5,13},{9,1},{13,5},{2,10},{6,14},... | collective-permute-start | bytes 192008 | tf_op jit(solution)/shard_map/ppermute | solution.py:358
  28.1 9.0 %collective-permute-start.5 = (bf16[16,2000]{1,0:T(8,128)(2,1)S(1)}, bf16[16,2000]{1,0:T(8,128)(2,1)S(1)}, u32[]{:S(2)}, u32[]{:S(2)}) collective-permute-start(bf16[16,2000]{1,0:T(8,128)(2,1)S(1)} %get-tuple-element.30), channel_id=1, source_target_pairs={{0,12},{4,8},{8,4},{12,0},{1,13},{5,9},{9,5},{13,1},{2,14},{6,10},... | collective-permute-start | bytes 192008 | tf_op jit(solution)/shard_map/ppermute | solution.py:358
  31.2 9.2 %collective-permute-start.7 = (bf16[24,2000]{1,0:T(8,128)(2,1)S(1)}, bf16[24,2000]{1,0:T(8,128)(2,1)S(1)}, u32[]{:S(2)}, u32[]{:S(2)}) collective-permute-start(bf16[24,2000]{1,0:T(8,128)(2,1)S(1)} %shard_map.79), channel_id=1, source_target_pairs={{0,8},{4,12},{8,0},{12,4},{1,9},{5,13},{9,1},{13,5},{2,10},{6,14},... | collective-permute-start | bytes 288008 | tf_op jit(solution)/shard_map/ppermute | solution.py:358
where the time goes:
time: 41.7 us; the launch traced here: 41.5 us
  waiting for transfers between devices  18.8 us (45%)
  starting transfers between devices  11.2 us (27%)
  Pallas kernels  10.9 us (26%)
  between operations  0.74 us (2%)
    ppermute x8, waiting for transfers between devices, swapped(): lax.ppermute(x, axis, [(i, i ^ bits) for i in range(lax.axis_size(axis))])  18.8 us
    ppermute x8, starting transfers between devices, swapped(): lax.ppermute(x, axis, [(i, i ^ bits) for i in range(lax.axis_size(axis))])  11.2 us
    pallas_call x5, Pallas kernels, call(): pl.pallas_call(kernel, out_shape=out_shape, in_specs=[smem if x.ndim == 1...  6.67 us
    pallas_call x1, Pallas kernels, crossing(): pl.pallas_call(functools.partial(crossing_kernel, groups), out_shape=[jax...  2.75 us
    pallas_call x1, Pallas kernels, staying(): pl.pallas_call(functools.partial(staying_kernel, groups), out_shape=[jax....  1.44 us
  transfers between devices with their start and end apart: 8, of which 3 were waited for; matrix products, arithmetic and copies ran while one was open for 0% of the time, Pallas kernels for 23%

commit v1 on v0

--- a/solution.py
+++ b/solution.py
@@ -211,16 +211,24 @@
         out_ref[r * height : (r + 1) * height, :] = packed_ref[:, r * width : (r + 1) * width]
 
 
-def share_of(rank, norb, ways):
+def share_of(green_ref, wide_ref, rank, ways):
+    norb = green_ref.shape[2]
     width = norb // ways
-    offsets = [w * width % LANES for w in range(ways)]
     begin = rank * width // LANES * LANES
-    return pl.ds(pl.multiple_of(begin, LANES), width + max(offsets)), rank * width - begin
+    size = window_size(norb, ways)
+    window = pl.ds(pl.multiple_of(begin, LANES), size)
+    wide_ref[:, :size] = green_ref[0, :, window].astype(F32)
+    moved = pltpu.roll(wide_ref[...], wide_ref.shape[1] - (rank * width - begin), 1)
+    return moved[:, :width].astype(BF16)
 
 
 def window_size(norb, ways):
     width = norb // ways
     return width + max(w * width % LANES for w in range(ways))
+
+
+def window_scratch(nocc, norb, ways):
+    return pltpu.VMEM((nocc, -(-window_size(norb, ways) // LANES) * LANES), F32)
 
 
 def call(kernel, out_shape, args, flops, moved, **more):
@@ -245,95 +253,63 @@
     return call(pair_kernel, out, (kept, received), kept.size, 8 * kept.size)[0]
 
 
-def early_kernel(ways, cot_ref, chol_ref, hamil_ref, green_ref, near_ref, kernel_ref, *outs):
-    d_chol_ref, d_trial_ref = outs
+def early_kernel(ways, cot_ref, chol_ref, hamil_ref, green_ref, near_ref, kernel_ref, *refs):
+    d_chol_ref, d_trial_ref, own_ref, near_wide = refs
     rank = lax.axis_index("walk")
-    vectors, _, norb = chol_ref.shape
-    window, _ = share_of(rank, norb, ways)
-    flipped = [nt(near_ref[0], chol_ref[v]) for v in range(chol_ref.shape[0])]
+    vectors = range(chol_ref.shape[0])
+    flipped = [nt(near_ref[0], chol_ref[v]) for v in vectors]
+    own_share = share_of(green_ref, own_ref, rank, ways)
+    near_share = share_of(near_ref, near_wide, rank, ways)
     total = cot_ref[rank] * nt(hamil_ref[...], green_ref[0])
     d_trial_ref[...] = total + cot_ref[rank ^ 1] * nt(hamil_ref[...], near_ref[0])
-    for v in range(vectors):
-        own = nn(kernel_ref[v].T, green_ref[0, :, window])
+    for v in vectors:
+        own = nn(kernel_ref[v].T, own_share)
         near = kernel_of(flipped[v], cot_ref[rank ^ 1])
-        d_chol_ref[v] = own + nn(near, near_ref[0, :, window])
-
-
-def middle_kernel(bits, ways, cot_ref, chol_ref, hamil_ref, green_ref, *refs):
-    old_chol, old_trial, d_chol_ref, d_trial_ref = refs
-    rank = lax.axis_index("walk")
-    cot = cot_ref[rank ^ bits]
-    vectors, _, norb = chol_ref.shape
-    window, _ = share_of(rank, norb, ways)
-    flipped = [nt(green_ref[0], chol_ref[v]) for v in range(chol_ref.shape[0])]
-    d_trial_ref[...] = old_trial[...] + cot * nt(hamil_ref[...], green_ref[0])
-    for v in range(vectors):
-        kernel = kernel_of(flipped[v], cot)
-        d_chol_ref[v] = old_chol[v] + nn(kernel, green_ref[0, :, window])
-
-
-def walkers(kernel, ways, cot, chol, hamil, greens, *rest):
-    vectors, nocc, norb = chol.shape
-    size = window_size(norb, ways)
-    return call(
-        kernel,
-        [
-            jax.ShapeDtypeStruct((vectors, nocc, size), F32),
-            jax.ShapeDtypeStruct((hamil.shape[0], nocc), F32),
-        ],
-        (cot, chol, hamil, *greens, *rest),
-        2 * nocc * len(greens) * (nocc * vectors * (norb + size) + hamil.size),
-        2 * (chol.size + len(greens) * nocc * norb),
-    )
-
-
-def late_kernel(bits, ways, cot_ref, chol_ref, hamil_ref, green_ref, *refs):
+        d_chol_ref[v] = own + nn(near, near_share)
+
+
+def walker_kernel(bits, ways, cot_ref, chol_ref, hamil_ref, green_ref, *refs):
     old_chol, old_trial, d_chol_ref, d_trial_ref, wide_ref = refs
     rank = lax.axis_index("walk")
     cot = cot_ref[rank ^ bits]
-    vectors, _, norb = chol_ref.shape
-    window, offset = share_of(rank, norb, ways)
-    flipped = [nt(green_ref[0], chol_ref[v]) for v in range(vectors)]
+    vectors = range(chol_ref.shape[0])
+    flipped = [nt(green_ref[0], chol_ref[v]) for v in vectors]
+    share = share_of(green_ref, wide_ref, rank, ways)
     d_trial_ref[...] = old_trial[...] + cot * nt(hamil_ref[...], green_ref[0])
-    for v in range(vectors):
-        kernel = kernel_of(flipped[v], cot)
-        total = old_chol[v] + nn(kernel, green_ref[0, :, window])
-        wide_ref[v, :, : total.shape[1]] = total
-        moved = pltpu.roll(wide_ref[v], wide_ref.shape[2] - offset, 1)
-        d_chol_ref[v] = moved[:, : norb // ways]
-
-
-def late(bits, ways, cot, chol, hamil, green, old):
+    for v in vectors:
+        d_chol_ref[v] = old_chol[v] + nn(kernel_of(flipped[v], cot), share)
+
+
+def walkers(kernel, ways, cot, chol, hamil, greens, *rest):
     vectors, nocc, norb = chol.shape
-    wide = -(-window_size(norb, ways) // LANES) * LANES
-    shapes = [(vectors, nocc, norb // ways), (hamil.shape[0], nocc)]
+    width = norb // ways
+    trial = jax.ShapeDtypeStruct((hamil.shape[0], nocc), F32)
     return call(
-        functools.partial(late_kernel, bits, ways),
-        [jax.ShapeDtypeStruct(shape, F32) for shape in shapes],
-        (cot, chol, hamil, green, *old),
-        2 * nocc * (nocc * vectors * (norb + wide) + hamil.size),
-        2 * (chol.size + hamil.size + nocc * norb),
-        scratch_shapes=[pltpu.VMEM((vectors, nocc, wide), F32)],
+        kernel,
+        [jax.ShapeDtypeStruct((vectors, nocc, width), F32), trial],
+        (cot, chol, hamil, *greens, *rest),
+        2 * nocc * len(greens) * (nocc * vectors * (norb + width) + hamil.size),
+        2 * (chol.size + len(greens) * nocc * norb),
+        scratch_shapes=[window_scratch(nocc, norb, ways)] * len(greens),
     )
 
 
 def joined_kernel(groups, cut, chol_ref, trial_ref, *refs):
     own_ref, first_ref, second_ref, third_ref, pair_ref = refs[:5]
     green_out, chol_out, trial_out, sum_ref, d_green, sems = refs[5:]
-    copies = [
-        pltpu.make_async_copy(trial_ref, trial_out, sems.at[1]),
-        pltpu.make_async_copy(chol_ref, chol_out, sems.at[2]),
-    ]
-    for copy in copies:
-        copy.start()
+    chol_copy = pltpu.make_async_copy(chol_ref, chol_out, sems.at[1])
+    chol_copy.start()
+    trial_copy = pltpu.make_async_copy(trial_ref, trial_out, sems.at[2])
+    trial_copy.start()
     total = own_ref[...] + first_ref[...].astype(F32)
     sum_ref[:cut] = total[:cut] + second_ref[...].astype(F32) + third_ref[...].astype(F32)
     sum_ref[cut:] = total[cut:] + pair_ref[...].astype(F32)
     unpacked_rows(d_green.at[0], sum_ref, groups)
-    copies.append(pltpu.make_async_copy(d_green, green_out, sems.at[0]))
-    copies[-1].start()
-    for copy in copies:
-        copy.wait()
+    green_copy = pltpu.make_async_copy(d_green, green_out, sems.at[0])
+    green_copy.start()
+    chol_copy.wait()
+    trial_copy.wait()
+    green_copy.wait()
 
 
 def joined(groups, cut, d_chol, d_trial, own, received):
@@ -379,9 +355,10 @@
     same = (ways, energy_cot, chol, hamil)
     sums = walkers(early, *same, [green, near], kernels)
     other = swapped(far, "walk", 1)
-    middle = functools.partial(middle_kernel, 2, ways)
+    middle = functools.partial(walker_kernel, 2, ways)
     sums = walkers(middle, *same, [far], *sums)
-    sums = late(3, *same, other, sums)
+    late = functools.partial(walker_kernel, 3, ways)
+    sums = walkers(late, *same, [other], *sums)
     return tuple(joined(groups, cut, *sums, own, (first, second, third, both)))
 
 

time: 41.7 us -> 41.7 us (level)
  no operation moved by 1% of the time
where the time goes in v1:
time: 41.7 us; the launch traced here: 41.5 us
  waiting for transfers between devices  18.8 us (45%)
  starting transfers between devices  11.2 us (27%)
  Pallas kernels  10.8 us (26%)
  between operations  0.74 us (2%)
    ppermute x8, waiting for transfers between devices, swapped(): lax.ppermute(x, axis, [(i, i ^ bits) for i in range(lax.axis_size(axis))])  18.8 us
    ppermute x8, starting transfers between devices, swapped(): lax.ppermute(x, axis, [(i, i ^ bits) for i in range(lax.axis_size(axis))])  11.2 us
    pallas_call x5, Pallas kernels, call(): pl.pallas_call(kernel, out_shape=out_shape, in_specs=[smem if x.ndim == 1...  6.61 us
    pallas_call x1, Pallas kernels, crossing(): pl.pallas_call(functools.partial(crossing_kernel, groups), out_shape=[jax...  2.75 us
    pallas_call x1, Pallas kernels, staying(): pl.pallas_call(functools.partial(staying_kernel, groups), out_shape=[jax....  1.44 us
  transfers between devices with their start and end apart: 8, of which 3 were waited for; matrix products, arithmetic and copies ran while one was open for 0% of the time, Pallas kernels for 23%

profile of v1, /device:TPU:0, one launch (start us, length us, event | category | flops | bytes accessed | tf_op | source)
XLA Modules:
  0.0 41.5 jit_solution(5236094624557850257)
XLA Ops:
  0.6 0.0 copy-start.1
  0.6 0.0 copy-start
  0.6 3.0 %collective-permute-start = (bf16[1,200,1600]{2,1,0:T(8,128)(2,1)}, bf16[1,200,1600]{2,1,0:T(8,128)(2,1)S(1)}, u32[]{:S(2)}, u32[]{:S(2)}) collective-permute-start(bf16[1,200,1600]{2,1,0:T(8,128)(2,1)} %green_ref.1), channel_id=1, source_target_pairs={{0,2},{1,3},{2,0},{3,1},{4,6},{5,7},{6,4},{7,5},{8,10},{9,11},{10,... | collective-permute-start | bytes 1920008 | tf_op jit(solution)/shard_map/ppermute | solution.py:334
  3.7 0.0 collective-permute-start.2
  3.7 15.2 %collective-permute-done.green_ref = bf16[1,200,1600]{2,1,0:T(8,128)(2,1)S(1)} collective-permute-done((bf16[1,200,1600]{2,1,0:T(8,128)(2,1)}, bf16[1,200,1600]{2,1,0:T(8,128)(2,1)S(1)}, u32[]{:S(2)}, u32[]{:S(2)}) %collective-permute-start) | collective-permute-done | bytes 640032 | tf_op jit(solution)/shard_map/ppermute | solution.py:334
  18.8 0.0 collective-permute-start.1
  18.8 0.0 copy-done.1
  18.9 0.0 copy-done
  18.9 0.0 copy-start.2
  18.9 2.7 %crossing.1 = (bf16[16,2000]{1,0:T(8,128)(2,1)S(1)}, bf16[16,2000]{1,0:T(8,128)(2,1)S(1)}, f32[24,2000]{1,0:T(8,128)S(1)}, bf16[24,2000]{1,0:T(8,128)(2,1)S(1)},...) custom-call(f32[8,128]{1,0:T(8,128)S(1)} %opening.1.refs_0_, ...), custom_call_target="tpu_custom_call" | custom-call | flops 512000000 | bytes 3360000 | tf_op jit(solution)/shard_map/crossing/pallas_call | solution.py:168
  21.6 1.9 %collective-permute-start.6 = (bf16[24,2000]{1,0:T(8,128)(2,1)S(1)}, bf16[24,2000]{1,0:T(8,128)(2,1)S(1)}, u32[]{:S(2)}, u32[]{:S(2)}) collective-permute-start(bf16[24,2000]{1,0:T(8,128)(2,1)S(1)} %get-tuple-element.32), channel_id=1, source_target_pairs={{0,4},{4,0},{8,12},{12,8},{1,5},{5,1},{9,13},{13,9},{2,6},{6,2},{1... | collective-permute-start | bytes 288008 | tf_op jit(solution)/shard_map/ppermute | solution.py:334
  23.5 0.0 copy-done.2
  23.5 1.4 %staying.1 = (bf16[40,2000]{1,0:T(8,128)(2,1)S(1)}, f32[40,2000]{1,0:T(8,128)S(1)}) custom-call(f32[4]{0:T(128)S(1)} %copy-done.2, bf16[2,200,200]{2,1,0:T(8,128)(2,1)S(1)} %get-tuple-element.19.kernel_ref.refs_1_, bf16[2,200,1600]{2,1,0:T(8,128)(2,1)S(1)} %copy-done, bf16[400,200]{1,0:T(8,128)(2,1)S(1)} %get-tuple-element.26.refs_3_, ...), custom_call_target="tpu_custom_call" | custom-call | flops 256000000 | bytes 2720000 | tf_op jit(solution)/shard_map/staying/pallas_call | solution.py:192
  25.0 0.3 collective-permute-start.3
  25.2 2.8 %collective-permute-start.4 = (bf16[16,2000]{1,0:T(8,128)(2,1)S(1)}, bf16[16,2000]{1,0:T(8,128)(2,1)S(1)}, u32[]{:S(2)}, u32[]{:S(2)}) collective-permute-start(bf16[16,2000]{1,0:T(8,128)(2,1)S(1)} %get-tuple-element.29), channel_id=1, source_target_pairs={{0,8},{4,12},{8,0},{12,4},{1,9},{5,13},{9,1},{13,5},{2,10},{6,14},... | collective-permute-start | bytes 192008 | tf_op jit(solution)/shard_map/ppermute | solution.py:334
  28.1 0.0 collective-permute-done.6.received_ref
  28.1 3.1 %collective-permute-start.5 = (bf16[16,2000]{1,0:T(8,128)(2,1)S(1)}, bf16[16,2000]{1,0:T(8,128)(2,1)S(1)}, u32[]{:S(2)}, u32[]{:S(2)}) collective-permute-start(bf16[16,2000]{1,0:T(8,128)(2,1)S(1)} %get-tuple-element.30), channel_id=1, source_target_pairs={{0,12},{4,8},{8,4},{12,0},{1,13},{5,9},{9,5},{13,1},{2,14},{6,10},... | collective-permute-start | bytes 192008 | tf_op jit(solution)/shard_map/ppermute | solution.py:334
  31.2 0.0 collective-permute-done.2.near_ref
  31.2 0.1 collective-permute-start.7
  31.3 2.1 %shard_map.76 = (f32[2,200,400]{2,1,0:T(8,128)S(1)}, f32[400,200]{1,0:T(8,128)S(1)}) custom-call(f32[4]{0:T(128)S(1)} %copy-done.2, bf16[2,200,1600]{2,1,0:T(8,128)(2,1)S(1)} %copy-done, bf16[400,1600]{1,0:T(8,128)(2,1)S(1)} %get-tuple-element.18.hamil_ref.refs_4_, bf16[1,200,1600]{2,1,0:T(8,128)(2,1)S(1)} %copy-done.1, ...), custom_call_target="tpu_custom_call" | custom-call | flops 1152000000 | bytes 2560000 | tf_op jit(solution)/shard_map/pallas_call | solution.py:237
  33.4 1.6 %shard_map.77 = (f32[2,200,400]{2,1,0:T(8,128)S(1)}, f32[400,200]{1,0:T(8,128)S(1)}) custom-call(f32[4]{0:T(128)S(1)} %copy-done.2, bf16[2,200,1600]{2,1,0:T(8,128)(2,1)S(1)} %copy-done, bf16[400,1600]{1,0:T(8,128)(2,1)S(1)} %get-tuple-element.18.hamil_ref.refs_4_, bf16[1,200,1600]{2,1,0:T(8,128)(2,1)S(1)} %collective-permute-done.green_ref, ...), custom_call_target="tpu_custom_call" | custom-call | flops 576000000 | bytes 1920000 | tf_op jit(solution)/shard_map/pallas_call | solution.py:237
  35.0 0.0 collective-permute-done.1.green_ref
  35.0 1.6 %shard_map.78 = (f32[2,200,400]{2,1,0:T(8,128)S(1)}, f32[400,200]{1,0:T(8,128)S(1)}) custom-call(f32[4]{0:T(128)S(1)} %copy-done.2, bf16[2,200,1600]{2,1,0:T(8,128)(2,1)S(1)} %copy-done, bf16[400,1600]{1,0:T(8,128)(2,1)S(1)} %get-tuple-element.18.hamil_ref.refs_4_, bf16[1,200,1600]{2,1,0:T(8,128)(2,1)S(1)} %collective-permute-done.1.green_ref, ...), custom_call_target="tpu_custom_call" | custom-call | flops 576000000 | bytes 1920000 | tf_op jit(solution)/shard_map/pallas_call | solution.py:237
  36.7 0.0 collective-permute-done.4.refs_2_
  36.7 0.3 collective-permute-done.5.refs_3_
  37.0 0.0 collective-permute-done.3.refs_1_
  37.0 3.3 %collective-permute-done.7.refs_4_ = bf16[24,2000]{1,0:T(8,128)(2,1)S(1)} collective-permute-done((bf16[24,2000]{1,0:T(8,128)(2,1)S(1)}, bf16[24,2000]{1,0:T(8,128)(2,1)S(1)}, u32[]{:S(2)}, u32[]{:S(2)}) %collective-permute-start.7) | collective-permute-done | bytes 96032 | tf_op jit(solution)/shard_map/ppermute | solution.py:334
  40.4 1.2 %shard_map.80 = (f32[1,200,400]{2,1,0:T(8,128)}, f32[2,200,400]{2,1,0:T(8,128)}, f32[400,200]{1,0:T(8,128)}) custom-call(f32[2,200,400]{2,1,0:T(8,128)S(1)} %get-tuple-element.24.chol_ref, f32[400,200]{1,0:T(8,128)S(1)} %get-tuple-element.25.trial_ref, f32[40,2000]{1,0:T(8,128)S(1)} %get-tuple-element.27.refs_0_, ...), custom_call_target="tpu_custom_call" | custom-call | flops 320000 | bytes 1280000 | tf_op jit(solution)/shard_map/pallas_call | solution.py:237
  (2 shorter events, 0.0 us)
Async XLA Ops:
  0.6 18.2 %copy-start.1 = (bf16[1,200,1600]{2,1,0:T(8,128)(2,1)S(1)}, bf16[1,200,1600]{2,1,0:T(8,128)(2,1)}, u32[]{:S(2)}) copy-start(bf16[1,200,1600]{2,1,0:T(8,128)(2,1)} %green_ref.1) | copy-start | bytes 1920004
  0.6 18.2 %copy-start = (bf16[2,200,1600]{2,1,0:T(8,128)(2,1)S(1)}, bf16[2,200,1600]{2,1,0:T(8,128)(2,1)}, u32[]{:S(2)}) copy-start(bf16[2,200,1600]{2,1,0:T(8,128)(2,1)} %refs_2_.3) | copy-start | bytes 3840004
  0.6 18.2 %collective-permute-start = (bf16[1,200,1600]{2,1,0:T(8,128)(2,1)}, bf16[1,200,1600]{2,1,0:T(8,128)(2,1)S(1)}, u32[]{:S(2)}, u32[]{:S(2)}) collective-permute-start(bf16[1,200,1600]{2,1,0:T(8,128)(2,1)} %green_ref.1), channel_id=1, source_target_pairs={{0,2},{1,3},{2,0},{3,1},{4,6},{5,7},{6,4},{7,5},{8,10},{9,11},{10,... | collective-permute-start | bytes 1920008 | tf_op jit(solution)/shard_map/ppermute | solution.py:334
  3.7 27.5 %collective-permute-start.2 = (bf16[1,200,1600]{2,1,0:T(8,128)(2,1)}, bf16[1,200,1600]{2,1,0:T(8,128)(2,1)S(1)}, u32[]{:S(2)}, u32[]{:S(2)}) collective-permute-start(bf16[1,200,1600]{2,1,0:T(8,128)(2,1)} %green_ref.1), channel_id=1, source_target_pairs={{0,1},{1,0},{2,3},{3,2},{4,5},{5,4},{6,7},{7,6},{8,9},{9,8},{10,11... | collective-permute-start | bytes 1920008 | tf_op jit(solution)/shard_map/ppermute | solution.py:334
  18.8 16.2 %collective-permute-start.1 = (bf16[1,200,1600]{2,1,0:T(8,128)(2,1)S(1)}, bf16[1,200,1600]{2,1,0:T(8,128)(2,1)S(1)}, u32[]{:S(2)}, u32[]{:S(2)}) collective-permute-start(bf16[1,200,1600]{2,1,0:T(8,128)(2,1)S(1)} %collective-permute-done.green_ref), channel_id=1, source_target_pairs={{0,1},{1,0},{2,3},{3,2},{4,5},{5,4},{6,7},{7,6},{8,9},{9,8},{10,11... | collective-permute-start | bytes 1920008 | tf_op jit(solution)/shard_map/ppermute | solution.py:334
  18.9 4.7 %copy-start.2 = (f32[4]{0:T(128)S(1)}, f32[4]{0:T(128)}, u32[]{:S(2)}) copy-start(f32[4]{0:T(128)} %refs_0_.1) | copy-start | bytes 52
  21.6 6.4 %collective-permute-start.6 = (bf16[24,2000]{1,0:T(8,128)(2,1)S(1)}, bf16[24,2000]{1,0:T(8,128)(2,1)S(1)}, u32[]{:S(2)}, u32[]{:S(2)}) collective-permute-start(bf16[24,2000]{1,0:T(8,128)(2,1)S(1)} %get-tuple-element.32), channel_id=1, source_target_pairs={{0,4},{4,0},{8,12},{12,8},{1,5},{5,1},{9,13},{13,9},{2,6},{6,2},{1... | collective-permute-start | bytes 288008 | tf_op jit(solution)/shard_map/ppermute | solution.py:334
  25.0 12.1 %collective-permute-start.3 = (bf16[40,2000]{1,0:T(8,128)(2,1)S(1)}, bf16[40,2000]{1,0:T(8,128)(2,1)S(1)}, u32[]{:S(2)}, u32[]{:S(2)}) collective-permute-start(bf16[40,2000]{1,0:T(8,128)(2,1)S(1)} %get-tuple-element.28), channel_id=1, source_target_pairs={{0,4},{4,0},{8,12},{12,8},{1,5},{5,1},{9,13},{13,9},{2,6},{6,2},{1... | collective-permute-start | bytes 480008 | tf_op jit(solution)/shard_map/ppermute | solution.py:334
  25.2 11.4 %collective-permute-start.4 = (bf16[16,2000]{1,0:T(8,128)(2,1)S(1)}, bf16[16,2000]{1,0:T(8,128)(2,1)S(1)}, u32[]{:S(2)}, u32[]{:S(2)}) collective-permute-start(bf16[16,2000]{1,0:T(8,128)(2,1)S(1)} %get-tuple-element.29), channel_id=1, source_target_pairs={{0,8},{4,12},{8,0},{12,4},{1,9},{5,13},{9,1},{13,5},{2,10},{6,14},... | collective-permute-start | bytes 192008 | tf_op jit(solution)/shard_map/ppermute | solution.py:334
  28.1 9.0 %collective-permute-start.5 = (bf16[16,2000]{1,0:T(8,128)(2,1)S(1)}, bf16[16,2000]{1,0:T(8,128)(2,1)S(1)}, u32[]{:S(2)}, u32[]{:S(2)}) collective-permute-start(bf16[16,2000]{1,0:T(8,128)(2,1)S(1)} %get-tuple-element.30), channel_id=1, source_target_pairs={{0,12},{4,8},{8,4},{12,0},{1,13},{5,9},{9,5},{13,1},{2,14},{6,10},... | collective-permute-start | bytes 192008 | tf_op jit(solution)/shard_map/ppermute | solution.py:334
  31.2 9.2 %collective-permute-start.7 = (bf16[24,2000]{1,0:T(8,128)(2,1)S(1)}, bf16[24,2000]{1,0:T(8,128)(2,1)S(1)}, u32[]{:S(2)}, u32[]{:S(2)}) collective-permute-start(bf16[24,2000]{1,0:T(8,128)(2,1)S(1)} %shard_map.79), channel_id=1, source_target_pairs={{0,8},{4,12},{8,0},{12,4},{1,9},{5,13},{9,1},{13,5},{2,10},{6,14},... | collective-permute-start | bytes 288008 | tf_op jit(solution)/shard_map/ppermute | solution.py:334

commit v2 on v1

--- a/solution.py
+++ b/solution.py
@@ -147,14 +147,13 @@
     out_ref[...] = jnp.zeros_like(out_ref)
 
 
-def opening():
+def opening(flops):
     return pl.pallas_call(
         opening_kernel,
         out_shape=jax.ShapeDtypeStruct((SUBLANES, LANES), F32),
         out_specs=pl.BlockSpec(memory_space=pltpu.VMEM),
-        cost_estimate=pl.CostEstimate(flops=4 * 10**9, bytes_accessed=4096, transcendentals=0),
+        cost_estimate=pl.CostEstimate(flops=flops, bytes_accessed=4096, transcendentals=0),
         compiler_params=pltpu.CompilerParams(vmem_limit_bytes=MIB, has_side_effects=True),
-        name="opening",
     )()
 
 
@@ -268,8 +267,8 @@
         d_chol_ref[v] = own + nn(near, near_share)
 
 
-def walker_kernel(bits, ways, cot_ref, chol_ref, hamil_ref, green_ref, *refs):
-    old_chol, old_trial, d_chol_ref, d_trial_ref, wide_ref = refs
+def middle_kernel(bits, ways, cot_ref, chol_ref, hamil_ref, green_ref, *refs):
+    old_chol, old_trial, d_chol_ref, d_trial_ref, kernel_ref, wide_ref = refs
     rank = lax.axis_index("walk")
     cot = cot_ref[rank ^ bits]
     vectors = range(chol_ref.shape[0])
@@ -277,16 +276,55 @@
     share = share_of(green_ref, wide_ref, rank, ways)
     d_trial_ref[...] = old_trial[...] + cot * nt(hamil_ref[...], green_ref[0])
     for v in vectors:
-        d_chol_ref[v] = old_chol[v] + nn(kernel_of(flipped[v], cot), share)
-
-
-def walkers(kernel, ways, cot, chol, hamil, greens, *rest):
+        kernel = kernel_of(flipped[v], cot)
+        kernel_ref[v] = kernel
+        d_chol_ref[v] = old_chol[v] + nn(kernel, share)
+
+
+def trial_kernel(bits, ways, _, cot_ref, hamil_ref, green_ref, old_ref, *refs):
+    d_trial_ref, share_ref, wide_ref = refs
+    rank = lax.axis_index("walk")
+    d_trial_ref[...] = old_ref[...] + cot_ref[rank ^ bits] * nt(hamil_ref[...], green_ref[0])
+    share_ref[...] = share_of(green_ref, wide_ref, rank, ways)
+
+
+def trial_term(bits, ways, token, cot, hamil, green, old):
+    _, nocc, norb = green.shape
+    return call(
+        functools.partial(trial_kernel, bits, ways),
+        [shape_of(old), jax.ShapeDtypeStruct((nocc, norb // ways), BF16)],
+        (token, cot, hamil, green, old),
+        2 * nocc * hamil.size,
+        2 * (hamil.size + green.size),
+        scratch_shapes=[window_scratch(nocc, norb, ways)],
+    )
+
+
+def chol_kernel(kernel_ref, share_ref, old_ref, out_ref):
+    for v in range(kernel_ref.shape[0]):
+        out_ref[v] = old_ref[v] + nn(kernel_ref[v], share_ref[...])
+
+
+def chol_term(kernels, share, old):
+    return call(
+        chol_kernel,
+        [shape_of(old)],
+        (kernels, share, old),
+        2 * kernels.size * share.shape[1],
+        8 * old.size,
+    )[0]
+
+
+def walkers(kernel, ways, cot, chol, hamil, greens, *rest, passed=False):
     vectors, nocc, norb = chol.shape
     width = norb // ways
-    trial = jax.ShapeDtypeStruct((hamil.shape[0], nocc), F32)
     return call(
         kernel,
-        [jax.ShapeDtypeStruct((vectors, nocc, width), F32), trial],
+        [
+            jax.ShapeDtypeStruct((vectors, nocc, width), F32),
+            jax.ShapeDtypeStruct((hamil.shape[0], nocc), F32),
+        ]
+        + [jax.ShapeDtypeStruct((vectors, nocc, nocc), BF16)] * passed,
         (cot, chol, hamil, *greens, *rest),
         2 * nocc * len(greens) * (nocc * vectors * (norb + width) + hamil.size),
         2 * (chol.size + len(greens) * nocc * norb),
@@ -340,7 +378,7 @@
     groups = row_groups(nocc, norb // lax.axis_size("chol"))
     cut = nocc // groups * 2 // 5 // SUBLANES * SUBLANES
     far = swapped(green, "walk", 2)
-    token = opening()
+    token = opening(4 * 10**9)
     second, third, kept, paired, kernels, trial, hamil = crossing(
         groups, cut, token, energy_cot, green, chol, trial, hamil
     )
@@ -355,11 +393,14 @@
     same = (ways, energy_cot, chol, hamil)
     sums = walkers(early, *same, [green, near], kernels)
     other = swapped(far, "walk", 1)
-    middle = functools.partial(walker_kernel, 2, ways)
-    sums = walkers(middle, *same, [far], *sums)
-    late = functools.partial(walker_kernel, 3, ways)
-    sums = walkers(late, *same, [other], *sums)
-    return tuple(joined(groups, cut, *sums, own, (first, second, third, both)))
+    middle = functools.partial(middle_kernel, 2, ways)
+    d_chol, d_trial, kernels = walkers(middle, *same, [far], *sums, passed=True)
+    kernels = swapped(kernels, "walk", 1)
+    mark = opening(1000)
+    d_trial, share = trial_term(3, ways, mark, energy_cot, hamil, other, d_trial)
+    d_chol = chol_term(kernels, share, d_chol)
+    received = (first, second, third, both)
+    return tuple(joined(groups, cut, d_chol, d_trial, own, received))
 
 
 def solution(mesh):

time: 41.7 us -> 43.9 us (1.053)
  waiting for transfers between devices: 18.8 us -> 20.1 us
  starting transfers between devices: 11.2 us -> 12.3 us
    ppermute x8 -> x9, waiting for transfers between devices: 18.8 us -> 20.1 us  [swapped(): lax.ppermute(x, axis, [(i, i ^ bits) for i in range(lax.axis_size(axis))])]
    ppermute x8 -> x9, starting transfers between devices: 11.2 us -> 12.3 us  [swapped(): lax.ppermute(x, axis, [(i, i ^ bits) for i in range(lax.axis_size(axis))])]
    pallas_call x5 -> x6, Pallas kernels: 6.61 us -> 6.38 us  [call(): pl.pallas_call(kernel, out_shape=out_shape, in_specs=[smem if x.ndim == 1...]
  transfers between devices with their start and end apart: 8 -> 9, of which waited for: 3 -> 3; matrix products, arithmetic and copies ran while one was open for 0% -> 0% of each run, Pallas kernels for 23% -> 21%
where the time goes in v2:
time: 43.9 us; the launch traced here: 43.8 us
  waiting for transfers between devices  20.1 us (46%)
  starting transfers between devices  12.3 us (28%)
  Pallas kernels  10.6 us (24%)
  between operations  0.73 us (2%)
    ppermute x9, waiting for transfers between devices, swapped(): lax.ppermute(x, axis, [(i, i ^ bits) for i in range(lax.axis_size(axis))])  20.1 us
    ppermute x9, starting transfers between devices, swapped(): lax.ppermute(x, axis, [(i, i ^ bits) for i in range(lax.axis_size(axis))])  12.3 us
    pallas_call x6, Pallas kernels, call(): pl.pallas_call(kernel, out_shape=out_shape, in_specs=[smem if x.ndim == 1...  6.38 us
    pallas_call x1, Pallas kernels, crossing(): pl.pallas_call(functools.partial(crossing_kernel, groups), out_shape=[jax...  2.75 us
    pallas_call x1, Pallas kernels, staying(): pl.pallas_call(functools.partial(staying_kernel, groups), out_shape=[jax....  1.44 us
  transfers between devices with their start and end apart: 9, of which 3 were waited for; matrix products, arithmetic and copies ran while one was open for 0% of the time, Pallas kernels for 21%

profile of v2, /device:TPU:0, one launch (start us, length us, event | category | flops | bytes accessed | tf_op | source)
XLA Modules:
  0.0 43.8 jit_solution(2124889135008088792)
XLA Ops:
  0.6 0.0 copy-start.1
  0.6 0.0 copy-start
  0.6 3.0 %collective-permute-start = (bf16[1,200,1600]{2,1,0:T(8,128)(2,1)}, bf16[1,200,1600]{2,1,0:T(8,128)(2,1)S(1)}, u32[]{:S(2)}, u32[]{:S(2)}) collective-permute-start(bf16[1,200,1600]{2,1,0:T(8,128)(2,1)} %green_ref.1), channel_id=1, source_target_pairs={{0,2},{1,3},{2,0},{3,1},{4,6},{5,7},{6,4},{7,5},{8,10},{9,11},{10,... | collective-permute-start | bytes 1920008 | tf_op jit(solution)/shard_map/ppermute | solution.py:372
  3.7 0.0 collective-permute-start.1
  3.7 15.2 %collective-permute-done.green_ref = bf16[1,200,1600]{2,1,0:T(8,128)(2,1)S(1)} collective-permute-done((bf16[1,200,1600]{2,1,0:T(8,128)(2,1)}, bf16[1,200,1600]{2,1,0:T(8,128)(2,1)S(1)}, u32[]{:S(2)}, u32[]{:S(2)}) %collective-permute-start) | collective-permute-done | bytes 640032 | tf_op jit(solution)/shard_map/ppermute | solution.py:372
  18.8 0.0 collective-permute-start.3
  18.8 0.0 copy-done.1
  18.9 0.0 copy-done
  18.9 0.0 copy-start.2
  18.9 2.7 %crossing.1 = (bf16[16,2000]{1,0:T(8,128)(2,1)S(1)}, bf16[16,2000]{1,0:T(8,128)(2,1)S(1)}, f32[24,2000]{1,0:T(8,128)S(1)}, bf16[24,2000]{1,0:T(8,128)(2,1)S(1)},...) custom-call(f32[8,128]{1,0:T(8,128)S(1)} %shard_map.76.refs_0_, ...), custom_call_target="tpu_custom_call" | custom-call | flops 512000000 | bytes 3360000 | tf_op jit(solution)/shard_map/crossing/pallas_call | solution.py:167
  21.6 1.9 %collective-permute-start.7 = (bf16[24,2000]{1,0:T(8,128)(2,1)S(1)}, bf16[24,2000]{1,0:T(8,128)(2,1)S(1)}, u32[]{:S(2)}, u32[]{:S(2)}) collective-permute-start(bf16[24,2000]{1,0:T(8,128)(2,1)S(1)} %get-tuple-element.34), channel_id=1, source_target_pairs={{0,4},{4,0},{8,12},{12,8},{1,5},{5,1},{9,13},{13,9},{2,6},{6,2},{1... | collective-permute-start | bytes 288008 | tf_op jit(solution)/shard_map/ppermute | solution.py:372
  23.5 0.0 collective-permute-done.1.near_ref
  23.5 0.0 copy-done.2
  23.5 2.1 %shard_map.77 = (f32[2,200,400]{2,1,0:T(8,128)S(1)}, f32[400,200]{1,0:T(8,128)S(1)}) custom-call(f32[4]{0:T(128)S(1)} %copy-done.2, bf16[2,200,1600]{2,1,0:T(8,128)(2,1)S(1)} %copy-done, bf16[400,1600]{1,0:T(8,128)(2,1)S(1)} %get-tuple-element.19.hamil_ref.refs_4_, bf16[1,200,1600]{2,1,0:T(8,128)(2,1)S(1)} %copy-done.1, ...), custom_call_target="tpu_custom_call" | custom-call | flops 1152000000 | bytes 2560000 | tf_op jit(solution)/shard_map/pallas_call | solution.py:236
  25.7 1.7 %shard_map.78 = (f32[2,200,400]{2,1,0:T(8,128)S(1)}, f32[400,200]{1,0:T(8,128)S(1)}, bf16[2,200,200]{2,1,0:T(8,128)(2,1)S(1)}) custom-call(f32[4]{0:T(128)S(1)} %copy-done.2, bf16[2,200,1600]{2,1,0:T(8,128)(2,1)S(1)} %copy-done, bf16[400,1600]{1,0:T(8,128)(2,1)S(1)} %get-tuple-element.19.hamil_ref.refs_4_, ...), custom_call_target="tpu_custom_call" | custom-call | flops 576000000 | bytes 1920000 | tf_op jit(solution)/shard_map/pallas_call | solution.py:236
  27.3 0.3 collective-permute-start.2
  27.6 1.4 %staying.1 = (bf16[40,2000]{1,0:T(8,128)(2,1)S(1)}, f32[40,2000]{1,0:T(8,128)S(1)}) custom-call(f32[4]{0:T(128)S(1)} %copy-done.2, bf16[2,200,200]{2,1,0:T(8,128)(2,1)S(1)} %get-tuple-element.20.kernel_ref.refs_1_, bf16[2,200,1600]{2,1,0:T(8,128)(2,1)S(1)} %copy-done, bf16[400,200]{1,0:T(8,128)(2,1)S(1)} %get-tuple-element.28.refs_3_, ...), custom_call_target="tpu_custom_call" | custom-call | flops 256000000 | bytes 2720000 | tf_op jit(solution)/shard_map/staying/pallas_call | solution.py:191
  29.1 0.4 collective-permute-start.4
  29.4 0.0 collective-permute-done.7.received_ref
  29.5 2.8 %collective-permute-start.8 = (bf16[24,2000]{1,0:T(8,128)(2,1)S(1)}, bf16[24,2000]{1,0:T(8,128)(2,1)S(1)}, u32[]{:S(2)}, u32[]{:S(2)}) collective-permute-start(bf16[24,2000]{1,0:T(8,128)(2,1)S(1)} %shard_map.82), channel_id=1, source_target_pairs={{0,8},{4,12},{8,0},{12,4},{1,9},{5,13},{9,1},{13,5},{2,10},{6,14},... | collective-permute-start | bytes 288008 | tf_op jit(solution)/shard_map/ppermute | solution.py:372
  32.3 0.2 collective-permute-start.5
  32.5 0.0 collective-permute-done.3.green_ref
  32.5 3.7 %collective-permute-start.6 = (bf16[16,2000]{1,0:T(8,128)(2,1)S(1)}, bf16[16,2000]{1,0:T(8,128)(2,1)S(1)}, u32[]{:S(2)}, u32[]{:S(2)}) collective-permute-start(bf16[16,2000]{1,0:T(8,128)(2,1)S(1)} %get-tuple-element.32), channel_id=1, source_target_pairs={{0,12},{4,8},{8,4},{12,0},{1,13},{5,9},{9,5},{13,1},{2,14},{6,10},... | collective-permute-start | bytes 192008 | tf_op jit(solution)/shard_map/ppermute | solution.py:372
  36.2 1.1 %shard_map.80 = (f32[400,200]{1,0:T(8,128)S(1)}, bf16[200,400]{1,0:T(8,128)(2,1)S(1)}) custom-call(f32[8,128]{1,0:T(8,128)S(1)} %shard_map.79._, f32[4]{0:T(128)S(1)} %copy-done.2, bf16[400,1600]{1,0:T(8,128)(2,1)S(1)} %get-tuple-element.19.hamil_ref.refs_4_, bf16[1,200,1600]{2,1,0:T(8,128)(2,1)S(1)} %collective-permute-done.3.green_ref, ...), custom_call_target="tpu_custom_call" | custom-call | flops 256000000 | bytes 1920000 | tf_op jit(solution)/shard_map/pallas_call | solution.py:236
  37.3 0.0 collective-permute-done.2.kernel_ref
  37.3 0.3 shard_map.81.chol_ref
  37.6 0.8 %collective-permute-done.5.refs_2_ = bf16[16,2000]{1,0:T(8,128)(2,1)S(1)} collective-permute-done((bf16[16,2000]{1,0:T(8,128)(2,1)S(1)}, bf16[16,2000]{1,0:T(8,128)(2,1)S(1)}, u32[]{:S(2)}, u32[]{:S(2)}) %collective-permute-start.5) | collective-permute-done | bytes 64032 | tf_op jit(solution)/shard_map/ppermute | solution.py:372
  38.4 4.2 %collective-permute-done.6.refs_3_ = bf16[16,2000]{1,0:T(8,128)(2,1)S(1)} collective-permute-done((bf16[16,2000]{1,0:T(8,128)(2,1)S(1)}, bf16[16,2000]{1,0:T(8,128)(2,1)S(1)}, u32[]{:S(2)}, u32[]{:S(2)}) %collective-permute-start.6) | collective-permute-done | bytes 64032 | tf_op jit(solution)/shard_map/ppermute | solution.py:372
  42.6 0.0 collective-permute-done.4.refs_1_
  42.6 0.0 collective-permute-done.8.refs_4_
  42.6 1.2 %shard_map.83 = (f32[1,200,400]{2,1,0:T(8,128)}, f32[2,200,400]{2,1,0:T(8,128)}, f32[400,200]{1,0:T(8,128)}) custom-call(f32[2,200,400]{2,1,0:T(8,128)S(1)} %shard_map.81.chol_ref, f32[400,200]{1,0:T(8,128)S(1)} %get-tuple-element.27.trial_ref, f32[40,2000]{1,0:T(8,128)S(1)} %get-tuple-element.29.refs_0_, ...), custom_call_target="tpu_custom_call" | custom-call | flops 320000 | bytes 1280000 | tf_op jit(solution)/shard_map/pallas_call | solution.py:236
  (3 shorter events, 0.0 us)
Async XLA Ops:
  0.6 18.2 %copy-start.1 = (bf16[1,200,1600]{2,1,0:T(8,128)(2,1)S(1)}, bf16[1,200,1600]{2,1,0:T(8,128)(2,1)}, u32[]{:S(2)}) copy-start(bf16[1,200,1600]{2,1,0:T(8,128)(2,1)} %green_ref.1) | copy-start | bytes 1920004
  0.6 18.2 %copy-start = (bf16[2,200,1600]{2,1,0:T(8,128)(2,1)S(1)}, bf16[2,200,1600]{2,1,0:T(8,128)(2,1)}, u32[]{:S(2)}) copy-start(bf16[2,200,1600]{2,1,0:T(8,128)(2,1)} %refs_2_.3) | copy-start | bytes 3840004
  0.6 18.2 %collective-permute-start = (bf16[1,200,1600]{2,1,0:T(8,128)(2,1)}, bf16[1,200,1600]{2,1,0:T(8,128)(2,1)S(1)}, u32[]{:S(2)}, u32[]{:S(2)}) collective-permute-start(bf16[1,200,1600]{2,1,0:T(8,128)(2,1)} %green_ref.1), channel_id=1, source_target_pairs={{0,2},{1,3},{2,0},{3,1},{4,6},{5,7},{6,4},{7,5},{8,10},{9,11},{10,... | collective-permute-start | bytes 1920008 | tf_op jit(solution)/shard_map/ppermute | solution.py:372
  3.7 19.8 %collective-permute-start.1 = (bf16[1,200,1600]{2,1,0:T(8,128)(2,1)}, bf16[1,200,1600]{2,1,0:T(8,128)(2,1)S(1)}, u32[]{:S(2)}, u32[]{:S(2)}) collective-permute-start(bf16[1,200,1600]{2,1,0:T(8,128)(2,1)} %green_ref.1), channel_id=1, source_target_pairs={{0,1},{1,0},{2,3},{3,2},{4,5},{5,4},{6,7},{7,6},{8,9},{9,8},{10,11... | collective-permute-start | bytes 1920008 | tf_op jit(solution)/shard_map/ppermute | solution.py:372
  18.8 13.6 %collective-permute-start.3 = (bf16[1,200,1600]{2,1,0:T(8,128)(2,1)S(1)}, bf16[1,200,1600]{2,1,0:T(8,128)(2,1)S(1)}, u32[]{:S(2)}, u32[]{:S(2)}) collective-permute-start(bf16[1,200,1600]{2,1,0:T(8,128)(2,1)S(1)} %collective-permute-done.green_ref), channel_id=1, source_target_pairs={{0,1},{1,0},{2,3},{3,2},{4,5},{5,4},{6,7},{7,6},{8,9},{9,8},{10,11... | collective-permute-start | bytes 1920008 | tf_op jit(solution)/shard_map/ppermute | solution.py:372
  18.9 4.7 %copy-start.2 = (f32[4]{0:T(128)S(1)}, f32[4]{0:T(128)}, u32[]{:S(2)}) copy-start(f32[4]{0:T(128)} %refs_0_.1) | copy-start | bytes 52
  21.6 7.8 %collective-permute-start.7 = (bf16[24,2000]{1,0:T(8,128)(2,1)S(1)}, bf16[24,2000]{1,0:T(8,128)(2,1)S(1)}, u32[]{:S(2)}, u32[]{:S(2)}) collective-permute-start(bf16[24,2000]{1,0:T(8,128)(2,1)S(1)} %get-tuple-element.34), channel_id=1, source_target_pairs={{0,4},{4,0},{8,12},{12,8},{1,5},{5,1},{9,13},{13,9},{2,6},{6,2},{1... | collective-permute-start | bytes 288008 | tf_op jit(solution)/shard_map/ppermute | solution.py:372
  27.3 10.0 %collective-permute-start.2 = (bf16[2,200,200]{2,1,0:T(8,128)(2,1)S(1)}, bf16[2,200,200]{2,1,0:T(8,128)(2,1)S(1)}, u32[]{:S(2)}, u32[]{:S(2)}) collective-permute-start(bf16[2,200,200]{2,1,0:T(8,128)(2,1)S(1)} %get-tuple-element.23), channel_id=1, source_target_pairs={{0,1},{1,0},{2,3},{3,2},{4,5},{5,4},{6,7},{7,6},{8,9},{9,8},{10,11... | collective-permute-start | bytes 480008 | tf_op jit(solution)/shard_map/ppermute | solution.py:372
  29.1 13.5 %collective-permute-start.4 = (bf16[40,2000]{1,0:T(8,128)(2,1)S(1)}, bf16[40,2000]{1,0:T(8,128)(2,1)S(1)}, u32[]{:S(2)}, u32[]{:S(2)}) collective-permute-start(bf16[40,2000]{1,0:T(8,128)(2,1)S(1)} %get-tuple-element.30), channel_id=1, source_target_pairs={{0,4},{4,0},{8,12},{12,8},{1,5},{5,1},{9,13},{13,9},{2,6},{6,2},{1... | collective-permute-start | bytes 480008 | tf_op jit(solution)/shard_map/ppermute | solution.py:372
  29.5 13.1 %collective-permute-start.8 = (bf16[24,2000]{1,0:T(8,128)(2,1)S(1)}, bf16[24,2000]{1,0:T(8,128)(2,1)S(1)}, u32[]{:S(2)}, u32[]{:S(2)}) collective-permute-start(bf16[24,2000]{1,0:T(8,128)(2,1)S(1)} %shard_map.82), channel_id=1, source_target_pairs={{0,8},{4,12},{8,0},{12,4},{1,9},{5,13},{9,1},{13,5},{2,10},{6,14},... | collective-permute-start | bytes 288008 | tf_op jit(solution)/shard_map/ppermute | solution.py:372
  32.3 6.1 %collective-permute-start.5 = (bf16[16,2000]{1,0:T(8,128)(2,1)S(1)}, bf16[16,2000]{1,0:T(8,128)(2,1)S(1)}, u32[]{:S(2)}, u32[]{:S(2)}) collective-permute-start(bf16[16,2000]{1,0:T(8,128)(2,1)S(1)} %get-tuple-element.31), channel_id=1, source_target_pairs={{0,8},{4,12},{8,0},{12,4},{1,9},{5,13},{9,1},{13,5},{2,10},{6,14},... | collective-permute-start | bytes 192008 | tf_op jit(solution)/shard_map/ppermute | solution.py:372
  32.5 10.1 %collective-permute-start.6 = (bf16[16,2000]{1,0:T(8,128)(2,1)S(1)}, bf16[16,2000]{1,0:T(8,128)(2,1)S(1)}, u32[]{:S(2)}, u32[]{:S(2)}) collective-permute-start(bf16[16,2000]{1,0:T(8,128)(2,1)S(1)} %get-tuple-element.32), channel_id=1, source_target_pairs={{0,12},{4,8},{8,4},{12,0},{1,13},{5,9},{9,5},{13,1},{2,14},{6,10},... | collective-permute-start | bytes 192008 | tf_op jit(solution)/shard_map/ppermute | solution.py:372
